TPU v7x, 128 devices: a whole 4x4x4 slice. The times are simulated.
128 devices in a mesh: rows: 8 (over x, core), cols: 16 (over z, y).
Axes of the slice: x: 4, y: 4, z: 4, core: 2. Of those that a mesh axis runs over, the one named last changes fastest.
Arguments:
- blocks: bfloat16 [96, 96, 256, 256], P('rows', 'cols'), may hold values from -1.5 to 1.5
- pattern: int32 [96, 96], P('rows', 'cols'), may hold values 0 or 1
- pivot_inverse: bfloat16 [2, 256, 256], replicated, may hold values from -0.375 to 0.375
- right_sides: float32 [96, 3, 256], P('rows'), may hold values from -6 to 6
Outputs:
- factored: bfloat16 [96, 96, 256, 256], P('rows', 'cols')
- forward: float32 [96, 3, 256], P('rows')
All inputs are finite; a program needn't handle non-finite values. No bound on the sum of `pattern` on one device may be relied on, other than what follows from the above.
Results may differ from a plain program's by a relative error of at most 0.0071.
Values may be sent and summed in bfloat16 or wider, within the bound.
A program may use at most 128 MiB of HBM per device.

v0:
```python
import jax
import jax.numpy as jnp
from jax import lax
from jax.sharding import PartitionSpec as P


def spread(x, axis, root):
    mine = lax.axis_index(axis) == root
    return lax.psum(jnp.where(mine, x, jnp.zeros_like(x)), axis)


def schur(part, lower, upper, live_part):
    prod = jnp.einsum("iab,jbc->ijac", lower, upper, preferred_element_type=jnp.float32)
    fresh = (part.astype(jnp.float32) - prod).astype(jnp.bfloat16)
    return jnp.where(live_part[:, :, None, None], fresh, part)


def on_device(blocks, pattern, pivot_inverse, right_sides):
    row_count = blocks.shape[0]
    nrows = lax.axis_size("rows")
    ncols = lax.axis_size("cols")
    row_glob = jnp.arange(row_count) * nrows + lax.axis_index("rows")
    col_glob = jnp.arange(blocks.shape[1]) * ncols + lax.axis_index("cols")
    live = pattern == 1
    zero_block = jnp.zeros((), jnp.bfloat16)
    matrix = jnp.where(live[:, :, None, None], blocks, zero_block)

    def column_panel(column, step):
        scaled = jnp.einsum(
            "nab,bc->nac", column, pivot_inverse[step], preferred_element_type=jnp.float32
        ).astype(jnp.bfloat16)
        landed = spread(scaled, "cols", step % ncols)
        return jnp.where((row_glob > step)[:, None, None], landed, zero_block)

    def pivot_panel(rowblocks, step):
        landed = spread(rowblocks, "rows", step % nrows)
        return jnp.where((col_glob > step)[:, None, None], landed, zero_block)

    def place_lower(matrix, lower, step):
        where_lower = (col_glob == step)[None, :] & (row_glob > step)[:, None]
        return jnp.where(where_lower[:, :, None, None], lower[:, None], matrix)

    lower_zero = column_panel(matrix[:, 0], 0)
    upper_zero = pivot_panel(matrix[0], 0)
    matrix = schur(matrix, lower_zero, upper_zero, live)
    lower_one = column_panel(matrix[:, 0], 1)
    upper_one = pivot_panel(matrix[0], 1)
    matrix = place_lower(matrix, lower_zero, 0)
    matrix = schur(matrix, lower_one, upper_one, live)
    matrix = place_lower(matrix, lower_one, 1)
    first = spread(right_sides[0], "rows", 0)
    rhs = right_sides - jnp.einsum(
        "nab,cb->nca", lower_zero.astype(jnp.float32), first, precision=lax.Precision.HIGHEST
    )
    second = spread(rhs[1 // nrows], "rows", 1 % nrows)
    rhs = rhs - jnp.einsum(
        "nab,cb->nca", lower_one.astype(jnp.float32), second, precision=lax.Precision.HIGHEST
    )
    return (matrix, rhs)


def solution(mesh):
    return jax.shard_map(
        on_device,
        mesh=mesh,
        in_specs=(P("rows", "cols", None, None), P("rows", "cols"), P(), P("rows", None, None)),
        out_specs=(P("rows", "cols", None, None), P("rows", None, None)),
        check_vma=False,
    )
```

profile of v0, /device:TPU:70, one launch (start us, length us, event | category | flops | bytes accessed | tf_op | source)
XLA Modules:
  0.0 359.7 jit_solution(4188063975407825787)
XLA Ops:
  7.2 0.7 broadcast_compare_fusion
  7.9 8.2 %copy_select_fusion = bf16[12,6,256,256]{3,2,0,1:T(8,128)(2,1)} fusion(bf16[12,6,256,256]{3,2,1,0:T(8,128)(2,1)} %param.4, pred[12,6]{0,1:T(8,128)(4,1)S(1)} %broadcast_compare_fusion), kind=kLoop, calls=%fused_computation.7 | loop fusion | flops 4718592 | bytes 18874440 | tf_op jit(solution)/shard_map/jit(_where)/select_n | solution.py:26
  16.1 3.1 broadcast_select_fusion.2
  19.2 0.0 all-reduce.5.cloned.1.call-start
  19.3 2.1 fusion.11
  21.4 0.0 all-reduce.9.cloned.1.call-start
  21.5 86.9 %all-reduce.7.cloned.1.call-done = bf16[12,256,256]{2,1,0:T(8,128)(2,1)} async-done(((bf16[12,256,256]{2,1,0:T(8,128)(2,1)}), bf16[12,256,256]{2,1,0:T(8,128)(2,1)}) %all-reduce.7.cloned.1.call-update) | async-done | bytes 1572880 | tf_op jit(solution)/shard_map/psum | solution.py:9
  108.4 1.6 broadcast_select_fusion
  110.0 61.4 %all-reduce.5.cloned.1.call-done = bf16[6,256,256]{2,1,0:T(8,128)(2,1)} async-done(((bf16[6,256,256]{2,1,0:T(8,128)(2,1)}), bf16[6,256,256]{2,1,0:T(8,128)(2,1)}) %all-reduce.5.cloned.1.call-update) | async-done | bytes 786448 | tf_op jit(solution)/shard_map/psum | solution.py:9
  171.4 6.5 %fusion.2 = bf16[12,6,256,256]{3,2,0,1:T(8,128)(2,1)S(1)} fusion(pred[12,6]{0,1:T(8,128)(4,1)S(1)} %broadcast_compare_fusion, bf16[12,256,256]{2,1,0:T(8,128)(2,1)S(1)} %broadcast_select_fusion, bf16[6,256,256]{2,1,0:T(8,128)(2,1)} %all-reduce.5.cloned.1.call-done, pred[6]{0:T(512)(128)(4,1)S(1)} %broadcast_compare_fusion.2, bf16[12,6,256,256]{3,2,1,0:T(8,128)(2,1)} %param.4), kind=kOutput, calls=%fused_computation.4 | convolution fusion | flops 2439905280 | bytes 21233742 | tf_op jit(solution)/shard_map/iab,jbc->ijac/dot_general | solution.py:13
  177.9 3.7 %copy-done = bf16[12,6,256,256]{3,2,0,1:T(8,128)(2,1)} copy-done((bf16[12,6,256,256]{3,2,0,1:T(8,128)(2,1)}, bf16[12,6,256,256]{3,2,0,1:T(8,128)(2,1)S(1)}, u32[]{:S(2)}) %copy-start) | copy-done | bytes 9437208
  181.6 1.7 broadcast_select_fusion.3
  183.4 11.7 %psum.46 = f32[3,256]{1,0:T(4,128)S(1)} all-reduce(f32[3,256]{1,0:T(4,128)S(1)} %select_bitcast_fusion), channel_id=1, replica_groups=mesh['rows'=8,'cols'=16] {'rows'}, use_global_device_ids=true, to_apply=%region_4.5 | all-reduce | flops 768 | bytes 6144 | tf_op jit(solution)/shard_map/psum | solution.py:9
  195.1 0.1 broadcast_and_fusion
  195.2 0.1 broadcast_and_fusion.1
  195.3 1.3 fusion.8
  196.6 13.0 %psum.47 = f32[3,256]{1,0:T(4,128)S(1)} all-reduce(f32[3,256]{1,0:T(4,128)S(1)} %fusion.24), channel_id=1, replica_groups=mesh['rows'=8,'cols'=16] {'rows'}, use_global_device_ids=true, to_apply=%region_5.6 | all-reduce | flops 768 | bytes 6144 | tf_op jit(solution)/shard_map/psum | solution.py:9
  209.6 2.1 fusion.9
  211.7 60.8 %all-reduce.9.cloned.1.call-done = bf16[12,256,256]{2,1,0:T(8,128)(2,1)} async-done(((bf16[12,256,256]{2,1,0:T(8,128)(2,1)}), bf16[12,256,256]{2,1,0:T(8,128)(2,1)}) %all-reduce.9.cloned.1.call-update) | async-done | bytes 1572880 | tf_op jit(solution)/shard_map/psum | solution.py:9
  272.5 1.6 broadcast_select_fusion.1
  274.0 2.0 fusion.7
  276.0 59.3 %all-reduce.11.cloned.1.call-done = bf16[6,256,256]{2,1,0:T(8,128)(2,1)} async-done(((bf16[6,256,256]{2,1,0:T(8,128)(2,1)}), bf16[6,256,256]{2,1,0:T(8,128)(2,1)}) %all-reduce.11.cloned.1.call-update) | async-done | bytes 786448 | tf_op jit(solution)/shard_map/psum | solution.py:9
  335.3 9.3 %fusion.4 = bf16[12,6,256,256]{3,2,0,1:T(8,128)(2,1)} fusion(bf16[12,6,256,256]{3,2,0,1:T(8,128)(2,1)} %copy-done, pred[12,6]{0,1:T(8,128)(4,1)S(1)} %broadcast_and_fusion, pred[12,6]{0,1:T(8,128)(4,1)S(1)} %broadcast_compare_fusion, pred[12,6]{0,1:T(8,128)(4,1)S(1)} %broadcast_and_fusion.1, bf16[12,256,256]{2,1,0:T(8,128)(2,1)S(1)} %broadcast_select_fusion, ...), kind=kOutput, calls=%fused_computation.6 | convolution fusion | flops 2444623872 | bytes 22806750 | tf_op jit(solution)/shard_map/iab,jbc->ijac/dot_general | solution.py:13
  344.6 8.6 %copy.13 = bf16[12,6,256,256]{3,2,1,0:T(8,128)(2,1)} copy(bf16[12,6,256,256]{3,2,0,1:T(8,128)(2,1)} %fusion.4) | data formatting | bytes 18874368
  (18 shorter events, 0.2 us)
Async XLA Ops:
  7.2 101.3 %all-reduce.7.cloned.1.call-start = ((), (), s32[]{:S(2)}) async-start(), calls=%async_computation.1 | async-start | bytes 3145728 | tf_op jit(solution)/shard_map/psum | solution.py:9
  7.9 8.2 %copy-start.2 = (bf16[2,256,256]{2,1,0:T(8,128)(2,1)S(1)}, bf16[2,256,256]{2,1,0:T(8,128)(2,1)}, u32[]{:S(2)}) copy-start(bf16[2,256,256]{2,1,0:T(8,128)(2,1)} %param.6) | copy-start | bytes 786436
  19.2 152.2 %all-reduce.5.cloned.1.call-start = ((), (), s32[]{:S(2)}) async-start(), calls=%async_computation | async-start | bytes 1572864 | tf_op jit(solution)/shard_map/psum | solution.py:9
  21.4 251.1 %all-reduce.9.cloned.1.call-start = ((), (), s32[]{:S(2)}) async-start(), calls=%async_computation.2 | async-start | bytes 3145728 | tf_op jit(solution)/shard_map/psum | solution.py:9
  177.9 3.7 %copy-start = (bf16[12,6,256,256]{3,2,0,1:T(8,128)(2,1)}, bf16[12,6,256,256]{3,2,0,1:T(8,128)(2,1)S(1)}, u32[]{:S(2)}) copy-start(bf16[12,6,256,256]{3,2,0,1:T(8,128)(2,1)S(1)} %fusion.2) | copy-start | bytes 28311556
  181.6 1.8 copy-start.1
  183.4 151.9 %all-reduce.11.cloned.1.call-start = ((), (), s32[]{:S(2)}) async-start(), calls=%async_computation.3 | async-start | bytes 1572864 | tf_op jit(solution)/shard_map/psum | solution.py:9
Sparse Core Ops, SparseCore 0:
  19.4 89.0 all-reduce.6
  110.8 60.5 all-reduce.4
  183.5 88.9 all-reduce.8
  274.7 60.5 all-reduce.10
where the time goes:
time: 363 us; the launch traced here: 360 us
  waiting for transfers between devices  268 us (74%)
  blocking collectives  24.6 us (7%)
  matrix products  23.9 us (7%)
  other arithmetic  16.4 us (5%)
  between operations  13.9 us (4%)
  local copies, waits for them, and re-layouts  12.3 us (3%)
    psum x4, waiting for transfers between devices, spread(): return lax.psum(jnp.where(mine, x, jnp.zeros_like(x)), axis)  268 us
    psum x2, blocking collectives, spread(): return lax.psum(jnp.where(mine, x, jnp.zeros_like(x)), axis)  24.6 us
    dot_general x2, matrix products, schur(): jnp.einsum('iab,jbc->ijac', lower, upper, preferred_element_type=jnp.floa...  15.8 us
    unnamed x7, local copies, waits for them, and re-layouts  12.3 us
    select_n x1, other arithmetic, on_device(): matrix = jnp.where(live[:, :, None, None], blocks, zero_block)  8.17 us
  transfers between devices with their start and end apart: 4, of which 4 were waited for; matrix products, arithmetic and copies ran while one was open for 3% of the time, Pallas kernels for 0%

commit v1 on v0

v1 whole, which is shorter than its diff:
```python
import functools

import jax
import jax.numpy as jnp
from jax import lax
from jax.experimental import pallas as pl
from jax.experimental.pallas import tpu as pltpu
from jax.sharding import PartitionSpec as P

MESH = pl.DeviceIdType.MESH
SIDE = 4

FORWARD = (
    (57344, 4864, 40705, 36864),
    (136, 34944, 16396, 17613),
    (3889, 48, 224, 2320),
    (70, 25671, 8194, 8736),
)
CHUNK = 64
LEAD = 2


def bit(table, position):
    return lax.rem(lax.shift_right_logical(jnp.int32(table), position), 2) == 1


def gather_kernel(
    blocks, pattern, rhs, panel, urow, pmask, umask, smask, ybuf,
    tree_send, tree_recv, local_sem, u_send, u_recv, sib_send, sib_recv,
    pm_send, pm_recv, tiny_send, tiny_recv, tsib_send, tsib_recv,
):
    row_blocks, col_blocks, side = blocks.shape[0], blocks.shape[1], blocks.shape[2]
    per = side // CHUNK
    steps = row_blocks * per // 4
    rows, cols = lax.axis_index("rows"), lax.axis_index("cols")
    x, core = rows // 2, lax.rem(rows, 2)
    z, y = cols // SIDE, lax.rem(cols, SIDE)
    other = 1 - core

    def at(new_x, new_core, new_z, new_y):
        return (new_x * 2 + new_core, new_z * SIDE + new_y)

    plane = (
        at(x, core, z, lax.rem(y + 1, SIDE)),
        at(x, core, lax.rem(z + 1, SIDE), y),
        at(x, core, z, lax.rem(y + 3, SIDE)),
        at(x, core, lax.rem(z + 3, SIDE), y),
    )
    along = at(lax.rem(x + 1 + 2 * core, SIDE), core, z, y)
    against = at(lax.rem(x + 3 + 2 * core, SIDE), core, z, y)
    sibling = at(x, other, z, y)
    hop = jnp.where(core == 0, x, lax.rem(SIDE - x, SIDE))
    head, passes = hop == 0, hop < SIDE - 1

    barrier = pltpu.get_barrier_semaphore()
    for peer in (*plane, along, against, sibling):
        pl.semaphore_signal(barrier, inc=1, device_id=peer, device_id_type=MESH)

    is_root, sends = [], []
    for p in range(2):
        position = lax.rem(y - p + SIDE, SIDE) * 4 + z
        is_root.append(cols == p)
        sends.append([[bit(FORWARD[k][d], position) for d in range(4)] for k in range(4)])
    pl.semaphore_wait(barrier, 7)

    def remote(src, dst, send, recv, to):
        return pltpu.make_async_remote_copy(
            src_ref=src, dst_ref=dst, send_sem=send, recv_sem=recv, device_id=to, device_id_type=MESH
        )

    def on_tree(p, k, src, dst, recv, send_of):
        for d in range(4):

            @pl.when(sends[p][k][d])
            def _():
                remote(src, dst, send_of(d), recv, plane[d]).start()

    def chunk_send(p, k, step, from_hbm):
        g = 4 * step + k
        dst = panel.at[p, g]
        if from_hbm:
            src = blocks.at[g // per, 0, pl.ds(pl.multiple_of(lax.rem(g, per) * CHUNK, CHUNK), CHUNK)]
        else:
            src = dst
        on_tree(p, k, src, dst, tree_recv.at[p, g], lambda d: tree_send.at[p, k, d])

    for p in range(2):

        @pl.when(is_root[p])
        def _():
            on_tree(p, 0, pattern, pmask.at[p], pm_recv.at[p], lambda d: pm_send.at[p, d])
            for step in range(LEAD):
                for k in range(4):
                    chunk_send(p, k, step, True)
            for i in range(row_blocks):
                for part in range(per):
                    pltpu.make_async_copy(
                        blocks.at[i, 0, pl.ds(part * CHUNK, CHUNK)], panel.at[p, i * per + part], local_sem.at[0]
                    ).start()
            pltpu.make_async_copy(pattern, pmask.at[p], local_sem.at[1]).start()

    @pl.when(head)
    def _():
        remote(pattern, umask.at[core], tiny_send.at[0, 0], tiny_recv.at[0], along).start()
        remote(pattern, umask.at[core], tsib_send.at[0], tsib_recv.at[0], sibling).start()
        remote(rhs.at[0], ybuf.at[core], tiny_send.at[0, 1], tiny_recv.at[1], along).start()
        remote(rhs.at[0], ybuf.at[core], tsib_send.at[1], tsib_recv.at[1], sibling).start()
        for j in range(col_blocks):
            remote(blocks.at[0, j], urow.at[core, j], u_send.at[j], u_recv.at[j], along).start()
            remote(blocks.at[0, j], urow.at[core, j], sib_send.at[j], sib_recv.at[j], sibling).start()
        for j in range(col_blocks):
            pltpu.make_async_copy(blocks.at[0, j], urow.at[core, j], local_sem.at[2]).start()
        pltpu.make_async_copy(pattern, umask.at[core], local_sem.at[3]).start()
        pltpu.make_async_copy(rhs.at[0], ybuf.at[core], local_sem.at[4]).start()

    for p in range(2):

        @pl.when(is_root[p])
        def _():
            whole = pltpu.make_async_copy(panel.at[p], panel.at[p], local_sem.at[0])
            whole.wait()
            pltpu.make_async_copy(pattern, pmask.at[p], local_sem.at[1]).wait()

        @pl.when(jnp.logical_not(is_root[p]))
        def _():
            remote(pattern, pmask.at[p], pm_send.at[p, 0], pm_recv.at[p], along).wait_recv()
            on_tree(p, 0, pmask.at[p], pmask.at[p], pm_recv.at[p], lambda d: pm_send.at[p, d])

    @pl.when(head)
    def _():
        for p in range(2):

            @pl.when(core == 1 - p)
            def _():
                remote(pmask.at[p], smask.at[core], tiny_send.at[0, 2], tiny_recv.at[2], along).start()
                remote(pmask.at[p], smask.at[core], tsib_send.at[2], tsib_recv.at[2], sibling).start()
                pltpu.make_async_copy(pmask.at[p], smask.at[core], local_sem.at[5]).start()

    def forward_tiny():
        for n, (src, dst) in enumerate(((umask, umask), (ybuf, ybuf), (smask, smask))):
            mine = dst.at[core]
            remote(mine, mine, tiny_send.at[0, n], tiny_recv.at[n], along).wait_recv()

            @pl.when(passes)
            def _():
                remote(mine, mine, tiny_send.at[0, n], tiny_recv.at[n], along).start()

            remote(mine, mine, tsib_send.at[n], tsib_recv.at[n], sibling).start()

    def forward_pivot(j):
        mine = urow.at[core, j]
        remote(mine, mine, u_send.at[j], u_recv.at[j], along).wait_recv()

        @pl.when(passes)
        def _():
            remote(mine, mine, u_send.at[j], u_recv.at[j], along).start()

        remote(mine, mine, sib_send.at[j], sib_recv.at[j], sibling).start()

    def one_step(step, carry):
        for p in range(2):

            @pl.when(jnp.logical_and(is_root[p], step + LEAD < steps))
            def _():
                for k in range(4):
                    chunk_send(p, k, step + LEAD, True)

        for k in range(4):
            for p in range(2):

                @pl.when(jnp.logical_not(is_root[p]))
                def _():
                    g = 4 * step + k
                    here = panel.at[p, g]
                    remote(here, here, tree_send.at[p, k, 0], tree_recv.at[p, g], along).wait_recv()
                    chunk_send(p, k, step, False)

        @pl.when(jnp.logical_and(head, step == 0))
        def _():
            for p in range(2):

                @pl.when(core == 1 - p)
                def _():
                    for part in range(per):
                        src = panel.at[p, part]
                        dst = urow.at[core, col_blocks, pl.ds(part * CHUNK, CHUNK)]
                        remote(src, dst, u_send.at[col_blocks + part], u_recv.at[col_blocks + part], along).start()
                        remote(src, dst, sib_send.at[col_blocks + part], sib_recv.at[col_blocks + part], sibling).start()
                        pltpu.make_async_copy(src, dst, local_sem.at[6]).start()

        @pl.when(jnp.logical_not(head))
        def _():
            @pl.when(step < col_blocks)
            def _():
                forward_pivot(step)

            @pl.when(step == col_blocks)
            def _():
                forward_tiny()
                for part in range(per):
                    mine = urow.at[core, col_blocks, pl.ds(part * CHUNK, CHUNK)]
                    n = col_blocks + part
                    remote(mine, mine, u_send.at[n], u_recv.at[n], along).wait_recv()

                    @pl.when(passes)
                    def _():
                        remote(mine, mine, u_send.at[n], u_recv.at[n], along).start()

                    remote(mine, mine, sib_send.at[n], sib_recv.at[n], sibling).start()

        return carry

    lax.fori_loop(0, steps, one_step, 0)

    for n, ref in enumerate((umask, ybuf, smask)):
        theirs = ref.at[other]
        remote(theirs, theirs, tsib_send.at[n], tsib_recv.at[n], sibling).wait_recv()
        remote(theirs, theirs, tsib_send.at[n], tsib_recv.at[n], sibling).wait_send()

        @pl.when(passes)
        def _():
            remote(theirs, theirs, tiny_send.at[0, n], tiny_recv.at[n], along).wait_send()

    for n in range(col_blocks + per):
        if n < col_blocks:
            theirs = urow.at[other, n]
        else:
            theirs = urow.at[other, col_blocks, pl.ds((n - col_blocks) * CHUNK, CHUNK)]
        remote(theirs, theirs, sib_send.at[n], sib_recv.at[n], sibling).wait_recv()
        remote(theirs, theirs, sib_send.at[n], sib_recv.at[n], sibling).wait_send()

        @pl.when(passes)
        def _():
            remote(theirs, theirs, u_send.at[n], u_recv.at[n], along).wait_send()

    @pl.when(head)
    def _():
        pltpu.make_async_copy(
            urow.at[core, pl.ds(0, col_blocks)], urow.at[core, pl.ds(0, col_blocks)], local_sem.at[2]
        ).wait()
        pltpu.make_async_copy(pattern, umask.at[core], local_sem.at[3]).wait()
        pltpu.make_async_copy(rhs.at[0], ybuf.at[core], local_sem.at[4]).wait()
        pltpu.make_async_copy(smask.at[core], smask.at[core], local_sem.at[5]).wait()
        pltpu.make_async_copy(urow.at[core, col_blocks], urow.at[core, col_blocks], local_sem.at[6]).wait()

    for p in range(2):
        for d in range(4):

            @pl.when(sends[p][0][d])
            def _():
                remote(pmask.at[p], pmask.at[p], pm_send.at[p, d], pm_recv.at[p], plane[d]).wait_send()

            for k in range(4):

                @pl.when(sends[p][k][d])
                def _():
                    part = panel.at[p, pl.ds(0, steps)]
                    remote(part, part, tree_send.at[p, k, d], tree_recv.at[p, 0], plane[d]).wait_send()


def gather(blocks, pattern, rhs):
    row_blocks, col_blocks, side = blocks.shape[:3]
    per = side // CHUNK
    dma = pltpu.SemaphoreType.DMA
    out_shape = (
        jax.ShapeDtypeStruct((2, row_blocks * per, CHUNK, side), jnp.bfloat16),
        jax.ShapeDtypeStruct((2, col_blocks + 1, side, side), jnp.bfloat16),
        jax.ShapeDtypeStruct((2, *pattern.shape), jnp.int32),
        jax.ShapeDtypeStruct((2, *pattern.shape), jnp.int32),
        jax.ShapeDtypeStruct((2, *pattern.shape), jnp.int32),
        jax.ShapeDtypeStruct((2, *rhs.shape[1:]), jnp.float32),
    )
    panel, urow, pmask, umask, smask, ybuf = pl.pallas_call(
        gather_kernel,
        out_shape=out_shape,
        in_specs=[pl.BlockSpec(memory_space=pl.ANY)] * 3,
        out_specs=[pl.BlockSpec(memory_space=pltpu.VMEM)] * 6,
        scratch_shapes=[
            dma((2, 4, 4)), dma((2, row_blocks * per)), dma((7,)),
            dma((col_blocks + per,)), dma((col_blocks + per,)),
            dma((col_blocks + per,)), dma((col_blocks + per,)),
            dma((2, 4)), dma((2,)), dma((1, 3)), dma((3,)), dma((3,)), dma((3,)),
        ],
        compiler_params=pltpu.CompilerParams(
            collective_id=0, has_side_effects=True, vmem_limit_bytes=16 * 2**20
        ),
        name="gather",
    )(blocks, pattern, rhs)
    return panel.reshape(2, row_blocks, side, side), urow, pmask, umask, smask, ybuf


def pieces(y):
    high = y.astype(jnp.bfloat16)
    rest = y - high.astype(jnp.float32)
    middle = rest.astype(jnp.bfloat16)
    low = (rest - middle.astype(jnp.float32)).astype(jnp.bfloat16)
    return high, middle, low


def matvec(stack, lower):
    return lax.dot_general(stack, lower, (((1,), (1,)), ((), ())), preferred_element_type=jnp.float32)


def update_kernel(
    pattern, pmask, umask, smask, blocks, panel, urow, pivots, ybuf, rhs, out, forward, upper, corner, ystack,
):
    i = pl.program_id(0)
    col_blocks, side = blocks.shape[1], blocks.shape[2]
    rows, cols = lax.axis_index("rows"), lax.axis_index("cols")
    row = i * 8 + rows
    f32, bf16 = jnp.float32, jnp.bfloat16

    def product(left, right):
        return jnp.dot(left, right, preferred_element_type=f32)

    def keep(flag, value):
        return jnp.where(flag, value, jnp.zeros_like(value))

    dirs = rhs.shape[1]

    @pl.when(i == 0)
    def _():
        corner[...] = keep(smask[0, 0, 0] == 1, urow[0, col_blocks])
        lower_one = product(keep(smask[1, 0, 0] == 1, urow[1, col_blocks]), pivots[0]).astype(bf16)
        for j in range(col_blocks):
            where = pl.ds(j * side, side)
            first = keep(jnp.logical_and(umask[0, 0, j] == 1, j * 16 + cols > 0), urow[0, j])
            second = (urow[1, j].astype(f32) - product(lower_one, first)).astype(bf16)
            upper[pl.ds(0, side), where] = first
            upper[pl.ds(side, side), where] = keep(
                jnp.logical_and(umask[1, 0, j] == 1, j * 16 + cols > 1), second
            )
        ystack[...] = jnp.zeros_like(ystack)
        for n, piece in enumerate(pieces(ybuf[0])):
            ystack[pl.ds(8 * n, dirs), pl.ds(0, side)] = piece.astype(f32)
        moved = matvec(ystack[:, pl.ds(0, side)].astype(bf16), lower_one)
        taken = moved[0:dirs] + moved[8 : 8 + dirs] + moved[16 : 16 + dirs]
        for n, piece in enumerate(pieces(ybuf[1] - taken)):
            ystack[pl.ds(8 * n, dirs), pl.ds(side, side)] = piece.astype(f32)

    first = product(panel[0, 0], pivots[0]).astype(bf16)
    first = keep(jnp.logical_and(pmask[0, i, 0] == 1, row > 0), first)
    schur = (panel[1, 0].astype(f32) - product(first, corner[...])).astype(bf16)
    second = product(schur, pivots[1]).astype(bf16)
    second = keep(jnp.logical_and(pmask[1, i, 0] == 1, row > 1), second)
    lower = jnp.concatenate([first, second], axis=1)
    for j in range(col_blocks):
        prod = product(lower, upper[:, pl.ds(j * side, side)])
        fresh = (blocks[0, j].astype(f32) - prod).astype(bf16)
        out[0, j] = keep(pattern[i, j] == 1, fresh)

    @pl.when(jnp.logical_and(cols == 0, row > 0))
    def _():
        out[0, 0] = first

    @pl.when(jnp.logical_and(cols == 1, row > 1))
    def _():
        out[0, 0] = second

    moved = matvec(ystack[...].astype(bf16), lower)
    forward[0] = rhs[0] - (moved[0:dirs] + moved[8 : 8 + dirs] + moved[16 : 16 + dirs])


def update(blocks, pattern, pivots, rhs, panel, urow, pmask, umask, smask, ybuf):
    row_blocks, col_blocks, side = blocks.shape[:3]
    dirs = rhs.shape[1]
    smem = pl.BlockSpec(memory_space=pltpu.SMEM)
    whole = lambda shape: pl.BlockSpec(shape, lambda i: (0,) * len(shape), pipeline_mode=pl.Buffered(1))
    return pl.pallas_call(
        update_kernel,
        grid=(row_blocks,),
        out_shape=(
            jax.ShapeDtypeStruct(blocks.shape, blocks.dtype),
            jax.ShapeDtypeStruct(rhs.shape, rhs.dtype),
        ),
        in_specs=[
            smem, smem, smem, smem,
            pl.BlockSpec((1, col_blocks, side, side), lambda i: (i, 0, 0, 0)),
            pl.BlockSpec((2, 1, side, side), lambda i: (0, i, 0, 0)),
            whole(urow.shape),
            whole(pivots.shape),
            whole(ybuf.shape),
            pl.BlockSpec((1, dirs, side), lambda i: (i, 0, 0)),
        ],
        out_specs=(
            pl.BlockSpec((1, col_blocks, side, side), lambda i: (i, 0, 0, 0)),
            pl.BlockSpec((1, dirs, side), lambda i: (i, 0, 0)),
        ),
        scratch_shapes=[
            pltpu.VMEM((2 * side, col_blocks * side), jnp.bfloat16),
            pltpu.VMEM((side, side), jnp.bfloat16),
            pltpu.VMEM((32, 2 * side), jnp.float32),
        ],
        compiler_params=pltpu.CompilerParams(vmem_limit_bytes=32 * 2**20),
        name="update",
    )(pattern, pmask, umask, smask, blocks, panel, urow, pivots, ybuf, rhs)


def on_device(blocks, pattern, pivot_inverse, right_sides):
    gathered = gather(blocks, pattern, right_sides)
    return update(blocks, pattern, pivot_inverse, right_sides, *gathered)


def solution(mesh):
    return jax.shard_map(
        on_device,
        mesh=mesh,
        in_specs=(P("rows", "cols", None, None), P("rows", "cols"), P(), P("rows", None, None)),
        out_specs=(P("rows", "cols", None, None), P("rows", None, None)),
        check_vma=False,
    )
```

time: 363 us -> 515 us (1.42)
  Pallas kernels: 0 us -> 504 us
  waiting for transfers between devices: 268 us -> 0 us
  blocking collectives: 24.6 us -> 0 us
  matrix products: 23.9 us -> 0 us
  other arithmetic: 16.4 us -> 0 us
  between operations: 13.9 us -> 0.67 us
  local copies, waits for them, and re-layouts: 12.3 us -> 6.21 us
    pallas_call x0 -> x2, Pallas kernels: none -> 504 us  [the longest x1 488 us: gather(): pl.pallas_call(gather_kernel, out_shape=out_shape, in_specs=[pl.BlockSpec...]
    psum x4 -> x0, waiting for transfers between devices: 268 us -> none  [spread(): return lax.psum(jnp.where(mine, x, jnp.zeros_like(x)), axis)]
    psum x2 -> x0, blocking collectives: 24.6 us -> none  [spread(): return lax.psum(jnp.where(mine, x, jnp.zeros_like(x)), axis)]
    dot_general x6 -> x0, matrix products: 23.9 us -> none  [the longest x2 15.8 us: schur(): jnp.einsum('iab,jbc->ijac', lower, upper, preferred_element_type=jnp.floa...]
    select_n x7 -> x0, other arithmetic: 15.5 us -> none  [the longest x1 8.17 us: on_device(): matrix = jnp.where(live[:, :, None, None], blocks, zero_block)]
    unnamed x7 -> x11, local copies, waits for them, and re-layouts: 12.3 us -> 6.21 us
  transfers between devices with their start and end apart: 4 -> 0, of which waited for: 4 -> 0; matrix products, arithmetic and copies ran while one was open for 3% -> 0% of each run, Pallas kernels for 0% -> 0%
where the time goes in v1:
time: 515 us; the launch traced here: 511 us
  Pallas kernels  504 us (98%)
  local copies, waits for them, and re-layouts  6.21 us (1%)
    pallas_call x1, Pallas kernels, gather(): pl.pallas_call(gather_kernel, out_shape=out_shape, in_specs=[pl.BlockSpec...  488 us
    pallas_call x1, Pallas kernels, update(): pl.pallas_call(update_kernel, grid=(row_blocks,), out_shape=(jax.ShapeDty...  16.6 us

profile of v1, /device:TPU:70, one launch (start us, length us, event | category | flops | bytes accessed | tf_op | source)
XLA Modules:
  0.0 511.2 jit_solution(4374708996874209128)
XLA Ops:
  0.6 0.8 copy.7.pattern
  1.4 0.0 copy-start
  1.4 3.7 copy-done
  5.1 0.0 copy-start.3
  5.1 0.8 copy-done.3
  5.9 0.0 copy-start.1
  5.9 0.0 copy-start.4
  5.9 487.7 %gather.1 = (bf16[2,48,64,256]{3,2,1,0:T(8,128)(2,1)S(1)}, bf16[2,7,256,256]{3,2,1,0:T(8,128)(2,1)S(1)}, s32[2,12,6]{2,1,0:T(8,128)S(1)}, s32[2,12,6]{2,1,0:T(8,...) custom-call(bf16[12,6,256,256]{3,2,1,0:T(8,128)(2,1)S(1)} %copy-done, s32[12,6]{1,0:T(8,128)S(1)} %copy.7.pattern, ...), custom_call_target="tpu_custom_call" | custom-call | tf_op jit(solution)/shard_map/gather/pallas_call | solution.py:273
  493.6 0.0 copy-done.1
  493.6 0.0 copy-done.4
  493.6 0.0 copy-start.2
  493.6 0.9 copy-done.2
  494.6 16.6 %update.1 = (bf16[12,6,256,256]{3,2,1,0:T(8,128)(2,1)}, f32[12,3,256]{2,1,0:T(4,128)}) custom-call(s32[12,6]{1,0:T(8,128)S(1)} %copy.7.pattern, s32[2,12,6]{2,1,0:T(8,128)S(1)} %get-tuple-element.8.pmask, s32[2,12,6]{2,1,0:T(8,128)S(1)} %get-tuple-element.9.umask, s32[2,12,6]{2,1,0:T(8,128)S(1)} %get-tuple-element.10.smask, ...), custom_call_target="tpu_custom_call" | custom-call | tf_op jit(solution)/shard_map/update/pallas_call | solution.py:369
Async XLA Ops:
  1.4 3.7 copy-start
  5.1 0.8 copy-start.3
  5.9 487.7 %copy-start.1 = (bf16[12,6,256,256]{3,2,1,0:T(8,128)(2,1)S(1)}, bf16[12,6,256,256]{3,2,1,0:T(8,128)(2,1)}, u32[]{:S(2)}) copy-start(bf16[12,6,256,256]{3,2,1,0:T(8,128)(2,1)} %blocks.3) | copy-start | bytes 28311556
  5.9 487.7 %copy-start.4 = (f32[12,3,256]{2,1,0:T(4,128)S(1)}, f32[12,3,256]{2,1,0:T(4,128)}, u32[]{:S(2)}) copy-start(f32[12,3,256]{2,1,0:T(4,128)} %rhs.3) | copy-start | bytes 110596
  493.6 1.0 copy-start.2

commit v2 on v1

--- a/solution.py
+++ b/solution.py
@@ -16,8 +16,12 @@
     (3889, 48, 224, 2320),
     (70, 25671, 8194, 8736),
 )
+DEPTH = ((23130, 60186, 1252), (23130, 55510, 10016), (23130, 7146, 58372), (23130, 29308, 36224))
+DEEPEST = 5
 CHUNK = 64
-LEAD = 2
+LAG = 3
+LAG_X = 2
+LATE_X = 4
 
 
 def bit(table, position):
@@ -56,10 +60,13 @@
     for peer in (*plane, along, against, sibling):
         pl.semaphore_signal(barrier, inc=1, device_id=peer, device_id_type=MESH)
 
-    is_root, sends = [], []
+    is_root, sends, depth = [], [], []
     for p in range(2):
         position = lax.rem(y - p + SIDE, SIDE) * 4 + z
         is_root.append(cols == p)
+        depth.append(
+            [sum(bit(DEPTH[k][b], position).astype(jnp.int32) << b for b in range(3)) for k in range(4)]
+        )
         sends.append([[bit(FORWARD[k][d], position) for d in range(4)] for k in range(4)])
     pl.semaphore_wait(barrier, 7)
 
@@ -88,10 +95,6 @@
 
         @pl.when(is_root[p])
         def _():
-            on_tree(p, 0, pattern, pmask.at[p], pm_recv.at[p], lambda d: pm_send.at[p, d])
-            for step in range(LEAD):
-                for k in range(4):
-                    chunk_send(p, k, step, True)
             for i in range(row_blocks):
                 for part in range(per):
                     pltpu.make_async_copy(
@@ -113,29 +116,6 @@
         pltpu.make_async_copy(pattern, umask.at[core], local_sem.at[3]).start()
         pltpu.make_async_copy(rhs.at[0], ybuf.at[core], local_sem.at[4]).start()
 
-    for p in range(2):
-
-        @pl.when(is_root[p])
-        def _():
-            whole = pltpu.make_async_copy(panel.at[p], panel.at[p], local_sem.at[0])
-            whole.wait()
-            pltpu.make_async_copy(pattern, pmask.at[p], local_sem.at[1]).wait()
-
-        @pl.when(jnp.logical_not(is_root[p]))
-        def _():
-            remote(pattern, pmask.at[p], pm_send.at[p, 0], pm_recv.at[p], along).wait_recv()
-            on_tree(p, 0, pmask.at[p], pmask.at[p], pm_recv.at[p], lambda d: pm_send.at[p, d])
-
-    @pl.when(head)
-    def _():
-        for p in range(2):
-
-            @pl.when(core == 1 - p)
-            def _():
-                remote(pmask.at[p], smask.at[core], tiny_send.at[0, 2], tiny_recv.at[2], along).start()
-                remote(pmask.at[p], smask.at[core], tsib_send.at[2], tsib_recv.at[2], sibling).start()
-                pltpu.make_async_copy(pmask.at[p], smask.at[core], local_sem.at[5]).start()
-
     def forward_tiny():
         for n, (src, dst) in enumerate(((umask, umask), (ybuf, ybuf), (smask, smask))):
             mine = dst.at[core]
@@ -157,30 +137,56 @@
 
         remote(mine, mine, sib_send.at[j], sib_recv.at[j], sibling).start()
 
-    def one_step(step, carry):
-        for p in range(2):
-
-            @pl.when(jnp.logical_and(is_root[p], step + LEAD < steps))
-            def _():
-                for k in range(4):
-                    chunk_send(p, k, step + LEAD, True)
-
+    def visit(p, k, step):
+        @pl.when(is_root[p])
+        def _():
+            if k == 0:
+
+                @pl.when(step == 0)
+                def _():
+                    on_tree(p, 0, pattern, pmask.at[p], pm_recv.at[p], lambda d: pm_send.at[p, d])
+
+            chunk_send(p, k, step, True)
+
+        @pl.when(jnp.logical_not(is_root[p]))
+        def _():
+            if k == 0:
+
+                @pl.when(step == 0)
+                def _():
+                    remote(pattern, pmask.at[p], pm_send.at[p, 0], pm_recv.at[p], along).wait_recv()
+                    on_tree(p, 0, pmask.at[p], pmask.at[p], pm_recv.at[p], lambda d: pm_send.at[p, d])
+
+            g = 4 * step + k
+            here = panel.at[p, g]
+            remote(here, here, tree_send.at[p, k, 0], tree_recv.at[p, g], along).wait_recv()
+            chunk_send(p, k, step, False)
+
+    corner_slot = LAG * DEEPEST + 1
+
+    def one_slot(slot, carry):
         for k in range(4):
             for p in range(2):
-
-                @pl.when(jnp.logical_not(is_root[p]))
-                def _():
-                    g = 4 * step + k
-                    here = panel.at[p, g]
-                    remote(here, here, tree_send.at[p, k, 0], tree_recv.at[p, g], along).wait_recv()
-                    chunk_send(p, k, step, False)
-
-        @pl.when(jnp.logical_and(head, step == 0))
+                step = slot - LAG * depth[p][k]
+
+                @pl.when(jnp.logical_and(step >= 0, step < steps))
+                def _():
+                    visit(p, k, step)
+
+        @pl.when(jnp.logical_and(head, slot == corner_slot))
         def _():
             for p in range(2):
 
+                @pl.when(is_root[p])
+                def _():
+                    pltpu.make_async_copy(panel.at[p], panel.at[p], local_sem.at[0]).wait()
+                    pltpu.make_async_copy(pattern, pmask.at[p], local_sem.at[1]).wait()
+
                 @pl.when(core == 1 - p)
                 def _():
+                    remote(pmask.at[p], smask.at[core], tiny_send.at[0, 2], tiny_recv.at[2], along).start()
+                    remote(pmask.at[p], smask.at[core], tsib_send.at[2], tsib_recv.at[2], sibling).start()
+                    pltpu.make_async_copy(pmask.at[p], smask.at[core], local_sem.at[5]).start()
                     for part in range(per):
                         src = panel.at[p, part]
                         dst = urow.at[core, col_blocks, pl.ds(part * CHUNK, CHUNK)]
@@ -190,11 +196,13 @@
 
         @pl.when(jnp.logical_not(head))
         def _():
-            @pl.when(step < col_blocks)
+            j = slot - LATE_X - LAG_X * hop
+
+            @pl.when(jnp.logical_and(j >= 0, j < col_blocks))
             def _():
-                forward_pivot(step)
-
-            @pl.when(step == col_blocks)
+                forward_pivot(j)
+
+            @pl.when(j == corner_slot - LATE_X)
             def _():
                 forward_tiny()
                 for part in range(per):
@@ -210,7 +218,15 @@
 
         return carry
 
-    lax.fori_loop(0, steps, one_step, 0)
+    slots = max(steps + LAG * DEEPEST, corner_slot + LAG_X * (SIDE - 1) + 1, LATE_X + col_blocks + LAG_X * (SIDE - 1))
+    lax.fori_loop(0, slots, one_slot, 0)
+
+    for p in range(2):
+
+        @pl.when(jnp.logical_and(is_root[p], jnp.logical_not(head)))
+        def _():
+            pltpu.make_async_copy(panel.at[p], panel.at[p], local_sem.at[0]).wait()
+            pltpu.make_async_copy(pattern, pmask.at[p], local_sem.at[1]).wait()
 
     for n, ref in enumerate((umask, ybuf, smask)):
         theirs = ref.at[other]
@@ -273,7 +289,7 @@
     panel, urow, pmask, umask, smask, ybuf = pl.pallas_call(
         gather_kernel,
         out_shape=out_shape,
-        in_specs=[pl.BlockSpec(memory_space=pl.ANY)] * 3,
+        in_specs=[pl.BlockSpec(memory_space=pltpu.HBM)] * 3,
         out_specs=[pl.BlockSpec(memory_space=pltpu.VMEM)] * 6,
         scratch_shapes=[
             dma((2, 4, 4)), dma((2, row_blocks * per)), dma((7,)),
@@ -301,14 +317,19 @@
     return lax.dot_general(stack, lower, (((1,), (1,)), ((), ())), preferred_element_type=jnp.float32)
 
 
+GROUP = 2
+
+
 def update_kernel(
-    pattern, pmask, umask, smask, blocks, panel, urow, pivots, ybuf, rhs, out, forward, upper, corner, ystack,
+    pattern, pmask, umask, smask, blocks, panel, urow, pivots, ybuf, rhs, out, forward, lower, upper, corner, ystack,
 ):
-    i = pl.program_id(0)
-    col_blocks, side = blocks.shape[1], blocks.shape[2]
+    j = pl.program_id(0)
+    row_blocks, side = blocks.shape[0], blocks.shape[2]
+    col_blocks = urow.shape[1] - 1
     rows, cols = lax.axis_index("rows"), lax.axis_index("cols")
-    row = i * 8 + rows
     f32, bf16 = jnp.float32, jnp.bfloat16
+    dirs = rhs.shape[1]
+    groups = [range(n, n + GROUP) for n in range(0, row_blocks, GROUP)]
 
     def product(left, right):
         return jnp.dot(left, right, preferred_element_type=f32)
@@ -316,78 +337,84 @@
     def keep(flag, value):
         return jnp.where(flag, value, jnp.zeros_like(value))
 
-    dirs = rhs.shape[1]
-
-    @pl.when(i == 0)
+    def part(group):
+        return pl.ds(group[0] * side, GROUP * side)
+
+    def stacked(p, group):
+        return panel[p, pl.ds(group[0], GROUP)].reshape(GROUP * side, side)
+
+    left, right = pl.ds(0, side), pl.ds(side, side)
+
+    @pl.when(j == 0)
     def _():
         corner[...] = keep(smask[0, 0, 0] == 1, urow[0, col_blocks])
+        for group in groups:
+            value = product(stacked(0, group), pivots[0]).astype(bf16)
+            for n, i in enumerate(group):
+                flag = jnp.logical_and(pmask[0, 0, i] == 1, i * 8 + rows > 0)
+                lower[pl.ds(i * side, side), left] = keep(flag, value[n * side : (n + 1) * side])
+        for group in groups:
+            value = stacked(1, group).astype(f32) - product(lower[part(group), left], corner[...])
+            lower[part(group), right] = value.astype(bf16)
+        for group in groups:
+            value = product(lower[part(group), right], pivots[1]).astype(bf16)
+            for n, i in enumerate(group):
+                flag = jnp.logical_and(pmask[1, 0, i] == 1, i * 8 + rows > 1)
+                lower[pl.ds(i * side, side), right] = keep(flag, value[n * side : (n + 1) * side])
         lower_one = product(keep(smask[1, 0, 0] == 1, urow[1, col_blocks]), pivots[0]).astype(bf16)
-        for j in range(col_blocks):
-            where = pl.ds(j * side, side)
-            first = keep(jnp.logical_and(umask[0, 0, j] == 1, j * 16 + cols > 0), urow[0, j])
-            second = (urow[1, j].astype(f32) - product(lower_one, first)).astype(bf16)
-            upper[pl.ds(0, side), where] = first
-            upper[pl.ds(side, side), where] = keep(
-                jnp.logical_and(umask[1, 0, j] == 1, j * 16 + cols > 1), second
-            )
+        for c in range(col_blocks):
+            first = keep(jnp.logical_and(umask[0, c, 0] == 1, c * 16 + cols > 0), urow[0, c])
+            second = (urow[1, c].astype(f32) - product(lower_one, first)).astype(bf16)
+            upper[c, left] = first
+            upper[c, right] = keep(jnp.logical_and(umask[1, c, 0] == 1, c * 16 + cols > 1), second)
         ystack[...] = jnp.zeros_like(ystack)
         for n, piece in enumerate(pieces(ybuf[0])):
-            ystack[pl.ds(8 * n, dirs), pl.ds(0, side)] = piece.astype(f32)
-        moved = matvec(ystack[:, pl.ds(0, side)].astype(bf16), lower_one)
+            ystack[pl.ds(8 * n, dirs), left] = piece.astype(f32)
+        moved = matvec(ystack[:, left].astype(bf16), lower_one)
         taken = moved[0:dirs] + moved[8 : 8 + dirs] + moved[16 : 16 + dirs]
         for n, piece in enumerate(pieces(ybuf[1] - taken)):
-            ystack[pl.ds(8 * n, dirs), pl.ds(side, side)] = piece.astype(f32)
-
-    first = product(panel[0, 0], pivots[0]).astype(bf16)
-    first = keep(jnp.logical_and(pmask[0, i, 0] == 1, row > 0), first)
-    schur = (panel[1, 0].astype(f32) - product(first, corner[...])).astype(bf16)
-    second = product(schur, pivots[1]).astype(bf16)
-    second = keep(jnp.logical_and(pmask[1, i, 0] == 1, row > 1), second)
-    lower = jnp.concatenate([first, second], axis=1)
-    for j in range(col_blocks):
-        prod = product(lower, upper[:, pl.ds(j * side, side)])
-        fresh = (blocks[0, j].astype(f32) - prod).astype(bf16)
-        out[0, j] = keep(pattern[i, j] == 1, fresh)
-
-    @pl.when(jnp.logical_and(cols == 0, row > 0))
-    def _():
-        out[0, 0] = first
-
-    @pl.when(jnp.logical_and(cols == 1, row > 1))
-    def _():
-        out[0, 0] = second
-
-    moved = matvec(ystack[...].astype(bf16), lower)
-    forward[0] = rhs[0] - (moved[0:dirs] + moved[8 : 8 + dirs] + moved[16 : 16 + dirs])
+            ystack[pl.ds(8 * n, dirs), right] = piece.astype(f32)
+        for i in range(row_blocks):
+            moved = matvec(ystack[...].astype(bf16), lower[pl.ds(i * side, side)])
+            forward[i] = rhs[i] - (moved[0:dirs] + moved[8 : 8 + dirs] + moved[16 : 16 + dirs])
+
+    for group in groups:
+        prod = product(lower[part(group)], upper[j])
+        for n, i in enumerate(group):
+            fresh = (blocks[i, 0].astype(f32) - prod[n * side : (n + 1) * side]).astype(bf16)
+            out[i, 0] = keep(pattern[j, i] == 1, fresh)
+
+    for p in range(2):
+
+        @pl.when(jnp.logical_and(cols == p, j == 0))
+        def _():
+            for i in range(row_blocks):
+
+                @pl.when(i * 8 + rows > p)
+                def _():
+                    out[i, 0] = lower[pl.ds(i * side, side), pl.ds(p * side, side)]
 
 
 def update(blocks, pattern, pivots, rhs, panel, urow, pmask, umask, smask, ybuf):
     row_blocks, col_blocks, side = blocks.shape[:3]
-    dirs = rhs.shape[1]
     smem = pl.BlockSpec(memory_space=pltpu.SMEM)
-    whole = lambda shape: pl.BlockSpec(shape, lambda i: (0,) * len(shape), pipeline_mode=pl.Buffered(1))
+    whole = lambda shape: pl.BlockSpec(shape, lambda j: (0,) * len(shape), pipeline_mode=pl.Buffered(1))
+    column = pl.BlockSpec((row_blocks, 1, side, side), lambda j: (0, j, 0, 0))
     return pl.pallas_call(
         update_kernel,
-        grid=(row_blocks,),
+        grid=(col_blocks,),
         out_shape=(
             jax.ShapeDtypeStruct(blocks.shape, blocks.dtype),
             jax.ShapeDtypeStruct(rhs.shape, rhs.dtype),
         ),
         in_specs=[
-            smem, smem, smem, smem,
-            pl.BlockSpec((1, col_blocks, side, side), lambda i: (i, 0, 0, 0)),
-            pl.BlockSpec((2, 1, side, side), lambda i: (0, i, 0, 0)),
-            whole(urow.shape),
-            whole(pivots.shape),
-            whole(ybuf.shape),
-            pl.BlockSpec((1, dirs, side), lambda i: (i, 0, 0)),
+            smem, smem, smem, smem, column, whole(panel.shape), whole(urow.shape), whole(pivots.shape),
+            whole(ybuf.shape), whole(rhs.shape),
         ],
-        out_specs=(
-            pl.BlockSpec((1, col_blocks, side, side), lambda i: (i, 0, 0, 0)),
-            pl.BlockSpec((1, dirs, side), lambda i: (i, 0, 0)),
-        ),
+        out_specs=(column, pl.BlockSpec(rhs.shape, lambda j: (0, 0, 0))),
         scratch_shapes=[
-            pltpu.VMEM((2 * side, col_blocks * side), jnp.bfloat16),
+            pltpu.VMEM((row_blocks * side, 2 * side), jnp.bfloat16),
+            pltpu.VMEM((col_blocks, 2 * side, side), jnp.bfloat16),
             pltpu.VMEM((side, side), jnp.bfloat16),
             pltpu.VMEM((32, 2 * side), jnp.float32),
         ],
@@ -397,7 +424,9 @@
 
 
 def on_device(blocks, pattern, pivot_inverse, right_sides):
-    gathered = gather(blocks, pattern, right_sides)
+    pattern = pattern.T
+    in_hbm = lambda array: pltpu.with_memory_space_constraint(array, pltpu.HBM)
+    gathered = gather(in_hbm(blocks), in_hbm(pattern), in_hbm(right_sides))
     return update(blocks, pattern, pivot_inverse, right_sides, *gathered)
 
 

time: 515 us -> 52.5 us (0.10)
  Pallas kernels: 504 us -> 50.5 us
  local copies, waits for them, and re-layouts: 6.21 us -> 0.96 us
    pallas_call x1, Pallas kernels: 488 us -> 38.8 us  [gather(): pl.pallas_call(gather_kernel, out_shape=out_shape, in_specs=[pl.BlockSpec...]
    unnamed x11 -> x8, local copies, waits for them, and re-layouts: 6.21 us -> 0.96 us
where the time goes in v2:
time: 52.5 us; the launch traced here: 52.2 us
  Pallas kernels  50.5 us (96%)
  local copies, waits for them, and re-layouts  0.96 us (2%)
  between operations  0.69 us (1%)
    pallas_call x1, Pallas kernels, gather(): pl.pallas_call(gather_kernel, out_shape=out_shape, in_specs=[pl.BlockSpec...  38.8 us
    pallas_call x1, Pallas kernels, update(): pl.pallas_call(update_kernel, grid=(col_blocks,), out_shape=(jax.ShapeDty...  11.7 us

profile of v2, /device:TPU:70, one launch (start us, length us, event | category | flops | bytes accessed | tf_op | source)
XLA Modules:
  0.0 52.2 jit_solution(13123238207466302485)
XLA Ops:
  0.6 0.0 copy-start.2
  0.6 0.0 copy-start
  0.6 0.0 copy-start.3
  0.7 38.8 %gather.1 = (bf16[2,48,64,256]{3,2,1,0:T(8,128)(2,1)S(1)}, bf16[2,7,256,256]{3,2,1,0:T(8,128)(2,1)S(1)}, s32[2,6,12]{2,1,0:T(8,128)S(1)}, s32[2,6,12]{2,1,0:T(8,...) custom-call(bf16[12,6,256,256]{3,2,1,0:T(8,128)(2,1)} %blocks.3, s32[6,12]{1,0:T(8,128)} %bitcast.3, ...), custom_call_target="tpu_custom_call" | custom-call | tf_op jit(solution)/shard_map/gather/pallas_call | solution.py:289
  39.5 0.0 copy-done.2
  39.5 0.0 copy-done
  39.5 0.0 copy-done.3
  39.5 0.0 copy-start.1
  39.5 0.9 %copy-done.1 = bf16[2,256,256]{2,1,0:T(8,128)(2,1)S(1)} copy-done((bf16[2,256,256]{2,1,0:T(8,128)(2,1)S(1)}, bf16[2,256,256]{2,1,0:T(8,128)(2,1)}, u32[]{:S(2)}) %copy-start.1) | copy-done | bytes 262168
  40.5 11.7 %update.1 = (bf16[12,6,256,256]{3,2,1,0:T(8,128)(2,1)}, f32[12,3,256]{2,1,0:T(4,128)}) custom-call(s32[6,12]{1,0:T(8,128)S(1)} %bitcast.4, s32[2,6,12]{2,1,0:T(8,128)S(1)} %get-tuple-element.8.pmask, s32[2,6,12]{2,1,0:T(8,128)S(1)} %get-tuple-element.9.umask, s32[2,6,12]{2,1,0:T(8,128)S(1)} %get-tuple-element.10.smask, ...), custom_call_target="tpu_custom_call" | custom-call | tf_op jit(solution)/shard_map/update/pallas_call | solution.py:403
Async XLA Ops:
  0.6 38.9 %copy-start.2 = (f32[12,3,256]{2,1,0:T(4,128)S(1)}, f32[12,3,256]{2,1,0:T(4,128)}, u32[]{:S(2)}) copy-start(f32[12,3,256]{2,1,0:T(4,128)} %rhs.3) | copy-start | bytes 110596
  0.6 38.9 %copy-start = (bf16[12,6,256,256]{3,2,1,0:T(8,128)(2,1)S(1)}, bf16[12,6,256,256]{3,2,1,0:T(8,128)(2,1)}, u32[]{:S(2)}) copy-start(bf16[12,6,256,256]{3,2,1,0:T(8,128)(2,1)} %blocks.3) | copy-start | bytes 28311556
  0.6 38.9 %copy-start.3 = (s32[12,6]{0,1:T(8,128)S(1)}, s32[12,6]{0,1:T(8,128)}, u32[]{:S(2)}) copy-start(s32[12,6]{0,1:T(8,128)} %param.5) | copy-start | bytes 868
  39.5 1.0 %copy-start.1 = (bf16[2,256,256]{2,1,0:T(8,128)(2,1)S(1)}, bf16[2,256,256]{2,1,0:T(8,128)(2,1)}, u32[]{:S(2)}) copy-start(bf16[2,256,256]{2,1,0:T(8,128)(2,1)} %pivots.1) | copy-start | bytes 786436

commit v3 on v2

--- a/solution.py
+++ b/solution.py
@@ -11,12 +11,13 @@
 SIDE = 4
 
 FORWARD = (
-    (57344, 4864, 40705, 36864),
-    (136, 34944, 16396, 17613),
-    (3889, 48, 224, 2320),
-    (70, 25671, 8194, 8736),
+    ((34, 17511, 16390, 8736), (57344, 12288, 16129, 6400), (76, 34944, 32776, 50253), (3985, 784, 224, 144)),
+    ((3985, 784, 224, 144), (34, 17511, 16390, 8736), (57344, 12288, 16129, 6400), (76, 34944, 32776, 50253)),
 )
-DEPTH = ((23130, 60186, 1252), (23130, 55510, 10016), (23130, 7146, 58372), (23130, 29308, 36224))
+DEPTH = (
+    ((23130, 29308, 36224), (23130, 60186, 1252), (23130, 55510, 10016), (23130, 7146, 58372)),
+    ((23130, 7146, 58372), (23130, 29308, 36224), (23130, 60186, 1252), (23130, 55510, 10016)),
+)
 DEEPEST = 5
 CHUNK = 64
 LAG = 3
@@ -29,7 +30,7 @@
 
 
 def gather_kernel(
-    blocks, pattern, rhs, panel, urow, pmask, umask, smask, ybuf,
+    blocks, pattern, rhs, pivots_hbm, panel, urow, pmask, umask, smask, ybuf, pivots,
     tree_send, tree_recv, local_sem, u_send, u_recv, sib_send, sib_recv,
     pm_send, pm_recv, tiny_send, tiny_recv, tsib_send, tsib_recv,
 ):
@@ -56,6 +57,8 @@
     hop = jnp.where(core == 0, x, lax.rem(SIDE - x, SIDE))
     head, passes = hop == 0, hop < SIDE - 1
 
+    load_pivots = pltpu.make_async_copy(pivots_hbm, pivots, local_sem.at[7])
+    load_pivots.start()
     barrier = pltpu.get_barrier_semaphore()
     for peer in (*plane, along, against, sibling):
         pl.semaphore_signal(barrier, inc=1, device_id=peer, device_id_type=MESH)
@@ -65,9 +68,9 @@
         position = lax.rem(y - p + SIDE, SIDE) * 4 + z
         is_root.append(cols == p)
         depth.append(
-            [sum(bit(DEPTH[k][b], position).astype(jnp.int32) << b for b in range(3)) for k in range(4)]
+            [sum(bit(DEPTH[p][k][b], position).astype(jnp.int32) << b for b in range(3)) for k in range(4)]
         )
-        sends.append([[bit(FORWARD[k][d], position) for d in range(4)] for k in range(4)])
+        sends.append([[bit(FORWARD[p][k][d], position) for d in range(4)] for k in range(4)])
     pl.semaphore_wait(barrier, 7)
 
     def remote(src, dst, send, recv, to):
@@ -228,6 +231,8 @@
             pltpu.make_async_copy(panel.at[p], panel.at[p], local_sem.at[0]).wait()
             pltpu.make_async_copy(pattern, pmask.at[p], local_sem.at[1]).wait()
 
+    load_pivots.wait()
+
     for n, ref in enumerate((umask, ybuf, smask)):
         theirs = ref.at[other]
         remote(theirs, theirs, tsib_send.at[n], tsib_recv.at[n], sibling).wait_recv()
@@ -274,7 +279,7 @@
                     remote(part, part, tree_send.at[p, k, d], tree_recv.at[p, 0], plane[d]).wait_send()
 
 
-def gather(blocks, pattern, rhs):
+def gather(blocks, pattern, rhs, pivots):
     row_blocks, col_blocks, side = blocks.shape[:3]
     per = side // CHUNK
     dma = pltpu.SemaphoreType.DMA
@@ -285,14 +290,15 @@
         jax.ShapeDtypeStruct((2, *pattern.shape), jnp.int32),
         jax.ShapeDtypeStruct((2, *pattern.shape), jnp.int32),
         jax.ShapeDtypeStruct((2, *rhs.shape[1:]), jnp.float32),
+        jax.ShapeDtypeStruct(pivots.shape, pivots.dtype),
     )
-    panel, urow, pmask, umask, smask, ybuf = pl.pallas_call(
+    panel, urow, pmask, umask, smask, ybuf, pivots = pl.pallas_call(
         gather_kernel,
         out_shape=out_shape,
-        in_specs=[pl.BlockSpec(memory_space=pltpu.HBM)] * 3,
-        out_specs=[pl.BlockSpec(memory_space=pltpu.VMEM)] * 6,
+        in_specs=[pl.BlockSpec(memory_space=pltpu.HBM)] * 4,
+        out_specs=[pl.BlockSpec(memory_space=pltpu.VMEM)] * 7,
         scratch_shapes=[
-            dma((2, 4, 4)), dma((2, row_blocks * per)), dma((7,)),
+            dma((2, 4, 4)), dma((2, row_blocks * per)), dma((8,)),
             dma((col_blocks + per,)), dma((col_blocks + per,)),
             dma((col_blocks + per,)), dma((col_blocks + per,)),
             dma((2, 4)), dma((2,)), dma((1, 3)), dma((3,)), dma((3,)), dma((3,)),
@@ -301,8 +307,8 @@
             collective_id=0, has_side_effects=True, vmem_limit_bytes=16 * 2**20
         ),
         name="gather",
-    )(blocks, pattern, rhs)
-    return panel.reshape(2, row_blocks, side, side), urow, pmask, umask, smask, ybuf
+    )(blocks, pattern, rhs, pivots)
+    return panel.reshape(2, row_blocks, side, side), urow, pmask, umask, smask, ybuf, pivots
 
 
 def pieces(y):
@@ -321,9 +327,9 @@
 
 
 def update_kernel(
-    pattern, pmask, umask, smask, blocks, panel, urow, pivots, ybuf, rhs, out, forward, lower, upper, corner, ystack,
+    pattern, pmask, umask, smask, blocks, panel, urow, pivots, ybuf, rhs, out, forward,
+    lower, upper, corner, ystack, solved, stage, out_sem, forward_sem,
 ):
-    j = pl.program_id(0)
     row_blocks, side = blocks.shape[0], blocks.shape[2]
     col_blocks = urow.shape[1] - 1
     rows, cols = lax.axis_index("rows"), lax.axis_index("cols")
@@ -345,80 +351,96 @@
 
     left, right = pl.ds(0, side), pl.ds(side, side)
 
-    @pl.when(j == 0)
-    def _():
-        corner[...] = keep(smask[0, 0, 0] == 1, urow[0, col_blocks])
+    corner[...] = keep(smask[0, 0, 0] == 1, urow[0, col_blocks])
+    for group in groups:
+        value = product(stacked(0, group), pivots[0]).astype(bf16)
+        for n, i in enumerate(group):
+            flag = jnp.logical_and(pmask[0, 0, i] == 1, i * 8 + rows > 0)
+            lower[pl.ds(i * side, side), left] = keep(flag, value[n * side : (n + 1) * side])
+    for group in groups:
+        value = stacked(1, group).astype(f32) - product(lower[part(group), left], corner[...])
+        lower[part(group), right] = value.astype(bf16)
+    for group in groups:
+        value = product(lower[part(group), right], pivots[1]).astype(bf16)
+        for n, i in enumerate(group):
+            flag = jnp.logical_and(pmask[1, 0, i] == 1, i * 8 + rows > 1)
+            lower[pl.ds(i * side, side), right] = keep(flag, value[n * side : (n + 1) * side])
+    lower_one = product(keep(smask[1, 0, 0] == 1, urow[1, col_blocks]), pivots[0]).astype(bf16)
+    for c in range(col_blocks):
+        first = keep(jnp.logical_and(umask[0, c, 0] == 1, c * 16 + cols > 0), urow[0, c])
+        second = (urow[1, c].astype(f32) - product(lower_one, first)).astype(bf16)
+        upper[c, left] = first
+        upper[c, right] = keep(jnp.logical_and(umask[1, c, 0] == 1, c * 16 + cols > 1), second)
+    ystack[...] = jnp.zeros_like(ystack)
+    for n, piece in enumerate(pieces(ybuf[0])):
+        ystack[pl.ds(8 * n, dirs), left] = piece.astype(f32)
+    moved = matvec(ystack[:, left].astype(bf16), lower_one)
+    taken = moved[0:dirs] + moved[8 : 8 + dirs] + moved[16 : 16 + dirs]
+    for n, piece in enumerate(pieces(ybuf[1] - taken)):
+        ystack[pl.ds(8 * n, dirs), right] = piece.astype(f32)
+    for i in range(row_blocks):
+        moved = matvec(ystack[...].astype(bf16), lower[pl.ds(i * side, side)])
+        solved[i] = rhs[i] - (moved[0:dirs] + moved[8 : 8 + dirs] + moved[16 : 16 + dirs])
+    send_forward = pltpu.make_async_copy(solved, forward, forward_sem)
+    send_forward.start()
+
+    def send(j, group):
+        rows_of = pl.ds(group[0], GROUP)
+        pltpu.make_async_copy(stage.at[j % 2, rows_of], out.at[rows_of, j], out_sem.at[j % 2]).start()
+
+    def sent(j):
+        pltpu.make_async_copy(stage.at[j % 2], out.at[:, j], out_sem.at[j % 2]).wait()
+
+    for j in range(col_blocks):
+        if j >= 2:
+            sent(j - 2)
         for group in groups:
-            value = product(stacked(0, group), pivots[0]).astype(bf16)
+            prod = product(lower[part(group)], upper[j])
             for n, i in enumerate(group):
-                flag = jnp.logical_and(pmask[0, 0, i] == 1, i * 8 + rows > 0)
-                lower[pl.ds(i * side, side), left] = keep(flag, value[n * side : (n + 1) * side])
-        for group in groups:
-            value = stacked(1, group).astype(f32) - product(lower[part(group), left], corner[...])
-            lower[part(group), right] = value.astype(bf16)
-        for group in groups:
-            value = product(lower[part(group), right], pivots[1]).astype(bf16)
-            for n, i in enumerate(group):
-                flag = jnp.logical_and(pmask[1, 0, i] == 1, i * 8 + rows > 1)
-                lower[pl.ds(i * side, side), right] = keep(flag, value[n * side : (n + 1) * side])
-        lower_one = product(keep(smask[1, 0, 0] == 1, urow[1, col_blocks]), pivots[0]).astype(bf16)
-        for c in range(col_blocks):
-            first = keep(jnp.logical_and(umask[0, c, 0] == 1, c * 16 + cols > 0), urow[0, c])
-            second = (urow[1, c].astype(f32) - product(lower_one, first)).astype(bf16)
-            upper[c, left] = first
-            upper[c, right] = keep(jnp.logical_and(umask[1, c, 0] == 1, c * 16 + cols > 1), second)
-        ystack[...] = jnp.zeros_like(ystack)
-        for n, piece in enumerate(pieces(ybuf[0])):
-            ystack[pl.ds(8 * n, dirs), left] = piece.astype(f32)
-        moved = matvec(ystack[:, left].astype(bf16), lower_one)
-        taken = moved[0:dirs] + moved[8 : 8 + dirs] + moved[16 : 16 + dirs]
-        for n, piece in enumerate(pieces(ybuf[1] - taken)):
-            ystack[pl.ds(8 * n, dirs), right] = piece.astype(f32)
-        for i in range(row_blocks):
-            moved = matvec(ystack[...].astype(bf16), lower[pl.ds(i * side, side)])
-            forward[i] = rhs[i] - (moved[0:dirs] + moved[8 : 8 + dirs] + moved[16 : 16 + dirs])
-
-    for group in groups:
-        prod = product(lower[part(group)], upper[j])
-        for n, i in enumerate(group):
-            fresh = (blocks[i, 0].astype(f32) - prod[n * side : (n + 1) * side]).astype(bf16)
-            out[i, 0] = keep(pattern[j, i] == 1, fresh)
-
-    for p in range(2):
-
-        @pl.when(jnp.logical_and(cols == p, j == 0))
-        def _():
-            for i in range(row_blocks):
-
-                @pl.when(i * 8 + rows > p)
-                def _():
-                    out[i, 0] = lower[pl.ds(i * side, side), pl.ds(p * side, side)]
-
-
-def update(blocks, pattern, pivots, rhs, panel, urow, pmask, umask, smask, ybuf):
+                fresh = (blocks[i, j].astype(f32) - prod[n * side : (n + 1) * side]).astype(bf16)
+                stage[j % 2, i] = keep(pattern[j, i] == 1, fresh)
+            if j > 0:
+                send(j, group)
+        if j == 0:
+            for p in range(2):
+
+                @pl.when(cols == p)
+                def _():
+                    for i in range(row_blocks):
+
+                        @pl.when(i * 8 + rows > p)
+                        def _():
+                            stage[0, i] = lower[pl.ds(i * side, side), pl.ds(p * side, side)]
+
+            for group in groups:
+                send(j, group)
+    sent(col_blocks - 2)
+    sent(col_blocks - 1)
+    send_forward.wait()
+
+
+def update(blocks, pattern, rhs, panel, urow, pmask, umask, smask, ybuf, pivots):
     row_blocks, col_blocks, side = blocks.shape[:3]
-    smem = pl.BlockSpec(memory_space=pltpu.SMEM)
-    whole = lambda shape: pl.BlockSpec(shape, lambda j: (0,) * len(shape), pipeline_mode=pl.Buffered(1))
-    column = pl.BlockSpec((row_blocks, 1, side, side), lambda j: (0, j, 0, 0))
+    smem, vmem = pl.BlockSpec(memory_space=pltpu.SMEM), pl.BlockSpec(memory_space=pltpu.VMEM)
     return pl.pallas_call(
         update_kernel,
-        grid=(col_blocks,),
         out_shape=(
             jax.ShapeDtypeStruct(blocks.shape, blocks.dtype),
             jax.ShapeDtypeStruct(rhs.shape, rhs.dtype),
         ),
-        in_specs=[
-            smem, smem, smem, smem, column, whole(panel.shape), whole(urow.shape), whole(pivots.shape),
-            whole(ybuf.shape), whole(rhs.shape),
-        ],
-        out_specs=(column, pl.BlockSpec(rhs.shape, lambda j: (0, 0, 0))),
+        in_specs=[smem] * 4 + [vmem] * 6,
+        out_specs=[pl.BlockSpec(memory_space=pltpu.HBM)] * 2,
         scratch_shapes=[
             pltpu.VMEM((row_blocks * side, 2 * side), jnp.bfloat16),
             pltpu.VMEM((col_blocks, 2 * side, side), jnp.bfloat16),
             pltpu.VMEM((side, side), jnp.bfloat16),
             pltpu.VMEM((32, 2 * side), jnp.float32),
+            pltpu.VMEM(rhs.shape, rhs.dtype),
+            pltpu.VMEM((2, row_blocks, side, side), jnp.bfloat16),
+            pltpu.SemaphoreType.DMA((2,)),
+            pltpu.SemaphoreType.DMA,
         ],
-        compiler_params=pltpu.CompilerParams(vmem_limit_bytes=32 * 2**20),
+        compiler_params=pltpu.CompilerParams(vmem_limit_bytes=24 * 2**20),
         name="update",
     )(pattern, pmask, umask, smask, blocks, panel, urow, pivots, ybuf, rhs)
 
@@ -426,8 +448,8 @@
 def on_device(blocks, pattern, pivot_inverse, right_sides):
     pattern = pattern.T
     in_hbm = lambda array: pltpu.with_memory_space_constraint(array, pltpu.HBM)
-    gathered = gather(in_hbm(blocks), in_hbm(pattern), in_hbm(right_sides))
-    return update(blocks, pattern, pivot_inverse, right_sides, *gathered)
+    gathered = gather(in_hbm(blocks), in_hbm(pattern), in_hbm(right_sides), in_hbm(pivot_inverse))
+    return tuple(update(blocks, pattern, right_sides, *gathered))
 
 
 def solution(mesh):

time: 52.5 us -> 49.5 us (0.943)
  Pallas kernels: 50.5 us -> 48.7 us
  local copies, waits for them, and re-layouts: 0.96 us -> 0.01 us
    pallas_call x1, Pallas kernels: 11.7 us -> 10.6 us  [update(): pl.pallas_call(update_kernel, out_shape=(jax.ShapeDtypeStruct(blocks.shap...]
    unnamed x8 -> x6, local copies, waits for them, and re-layouts: 0.96 us -> 0.01 us
    pallas_call x1, Pallas kernels: 38.8 us -> 38.1 us  [gather(): pl.pallas_call(gather_kernel, out_shape=out_shape, in_specs=[pl.BlockSpec...]
where the time goes in v3:
time: 49.5 us; the launch traced here: 49.4 us
  Pallas kernels  48.7 us (98%)
  between operations  0.69 us (1%)
    pallas_call x1, Pallas kernels, gather(): pl.pallas_call(gather_kernel, out_shape=out_shape, in_specs=[pl.BlockSpec...  38.1 us
    pallas_call x1, Pallas kernels, update(): pl.pallas_call(update_kernel, out_shape=(jax.ShapeDtypeStruct(blocks.shap...  10.6 us

profile of v3, /device:TPU:70, one launch (start us, length us, event | category | flops | bytes accessed | tf_op | source)
XLA Modules:
  0.0 49.4 jit_solution(4829073462770696867)
XLA Ops:
  0.6 0.0 copy-start.1
  0.6 0.0 copy-start
  0.7 0.0 copy-start.2
  0.7 38.1 %gather.1 = (bf16[2,48,64,256]{3,2,1,0:T(8,128)(2,1)S(1)}, bf16[2,7,256,256]{3,2,1,0:T(8,128)(2,1)S(1)}, s32[2,6,12]{2,1,0:T(8,128)S(1)}, s32[2,6,12]{2,1,0:T(8,...) custom-call(bf16[12,6,256,256]{3,2,1,0:T(8,128)(2,1)} %blocks.3, ...), custom_call_target="tpu_custom_call" | custom-call | tf_op jit(solution)/shard_map/gather/pallas_call | solution.py:295
  38.8 0.0 copy-done.1
  38.8 0.0 copy-done
  38.8 0.0 copy-done.2
  38.8 10.6 %update.1 = (bf16[12,6,256,256]{3,2,1,0:T(8,128)(2,1)}, f32[12,3,256]{2,1,0:T(4,128)}) custom-call(s32[6,12]{1,0:T(8,128)S(1)} %bitcast.4, s32[2,6,12]{2,1,0:T(8,128)S(1)} %get-tuple-element.9.pmask, s32[2,6,12]{2,1,0:T(8,128)S(1)} %get-tuple-element.10.umask, s32[2,6,12]{2,1,0:T(8,128)S(1)} %get-tuple-element.11.smask, ...), custom_call_target="tpu_custom_call" | custom-call | tf_op jit(solution)/shard_map/update/pallas_call | solution.py:425
Async XLA Ops:
  0.6 38.2 %copy-start.1 = (f32[12,3,256]{2,1,0:T(4,128)S(1)}, f32[12,3,256]{2,1,0:T(4,128)}, u32[]{:S(2)}) copy-start(f32[12,3,256]{2,1,0:T(4,128)} %rhs.3) | copy-start | bytes 110596
  0.6 38.2 %copy-start = (bf16[12,6,256,256]{3,2,1,0:T(8,128)(2,1)S(1)}, bf16[12,6,256,256]{3,2,1,0:T(8,128)(2,1)}, u32[]{:S(2)}) copy-start(bf16[12,6,256,256]{3,2,1,0:T(8,128)(2,1)} %blocks.3) | copy-start | bytes 28311556
  0.7 38.2 %copy-start.2 = (s32[12,6]{0,1:T(8,128)S(1)}, s32[12,6]{0,1:T(8,128)}, u32[]{:S(2)}) copy-start(s32[12,6]{0,1:T(8,128)} %param.5) | copy-start | bytes 868

commit v4 on v3

--- a/solution.py
+++ b/solution.py
@@ -378,12 +378,6 @@
     taken = moved[0:dirs] + moved[8 : 8 + dirs] + moved[16 : 16 + dirs]
     for n, piece in enumerate(pieces(ybuf[1] - taken)):
         ystack[pl.ds(8 * n, dirs), right] = piece.astype(f32)
-    for i in range(row_blocks):
-        moved = matvec(ystack[...].astype(bf16), lower[pl.ds(i * side, side)])
-        solved[i] = rhs[i] - (moved[0:dirs] + moved[8 : 8 + dirs] + moved[16 : 16 + dirs])
-    send_forward = pltpu.make_async_copy(solved, forward, forward_sem)
-    send_forward.start()
-
     def send(j, group):
         rows_of = pl.ds(group[0], GROUP)
         pltpu.make_async_copy(stage.at[j % 2, rows_of], out.at[rows_of, j], out_sem.at[j % 2]).start()
@@ -414,6 +408,11 @@
 
             for group in groups:
                 send(j, group)
+    for i in range(row_blocks):
+        moved = matvec(ystack[...].astype(bf16), lower[pl.ds(i * side, side)])
+        solved[i] = rhs[i] - (moved[0:dirs] + moved[8 : 8 + dirs] + moved[16 : 16 + dirs])
+    send_forward = pltpu.make_async_copy(solved, forward, forward_sem)
+    send_forward.start()
     sent(col_blocks - 2)
     sent(col_blocks - 1)
     send_forward.wait()

time: 49.5 us -> 49.3 us (level)
  no operation moved by 1% of the time
where the time goes in v4:
time: 49.3 us; the launch traced here: 49.2 us
  Pallas kernels  48.5 us (98%)
  between operations  0.69 us (1%)
    pallas_call x1, Pallas kernels, gather(): pl.pallas_call(gather_kernel, out_shape=out_shape, in_specs=[pl.BlockSpec...  38.1 us
    pallas_call x1, Pallas kernels, update(): pl.pallas_call(update_kernel, out_shape=(jax.ShapeDtypeStruct(blocks.shap...  10.4 us

profile of v4, /device:TPU:70, one launch (start us, length us, event | category | flops | bytes accessed | tf_op | source)
XLA Modules:
  0.0 49.2 jit_solution(14582492797049723039)
XLA Ops:
  0.6 0.0 copy-start.1
  0.6 0.0 copy-start
  0.7 0.0 copy-start.2
  0.7 38.1 %gather.1 = (bf16[2,48,64,256]{3,2,1,0:T(8,128)(2,1)S(1)}, bf16[2,7,256,256]{3,2,1,0:T(8,128)(2,1)S(1)}, s32[2,6,12]{2,1,0:T(8,128)S(1)}, s32[2,6,12]{2,1,0:T(8,...) custom-call(bf16[12,6,256,256]{3,2,1,0:T(8,128)(2,1)} %blocks.3, ...), custom_call_target="tpu_custom_call" | custom-call | tf_op jit(solution)/shard_map/gather/pallas_call | solution.py:295
  38.8 0.0 copy-done.1
  38.8 0.0 copy-done
  38.8 0.0 copy-done.2
  38.8 10.4 %update.1 = (bf16[12,6,256,256]{3,2,1,0:T(8,128)(2,1)}, f32[12,3,256]{2,1,0:T(4,128)}) custom-call(s32[6,12]{1,0:T(8,128)S(1)} %bitcast.4, s32[2,6,12]{2,1,0:T(8,128)S(1)} %get-tuple-element.9.pmask, s32[2,6,12]{2,1,0:T(8,128)S(1)} %get-tuple-element.10.umask, s32[2,6,12]{2,1,0:T(8,128)S(1)} %get-tuple-element.11.smask, ...), custom_call_target="tpu_custom_call" | custom-call | tf_op jit(solution)/shard_map/update/pallas_call | solution.py:424
Async XLA Ops:
  0.6 38.2 %copy-start.1 = (f32[12,3,256]{2,1,0:T(4,128)S(1)}, f32[12,3,256]{2,1,0:T(4,128)}, u32[]{:S(2)}) copy-start(f32[12,3,256]{2,1,0:T(4,128)} %rhs.3) | copy-start | bytes 110596
  0.6 38.2 %copy-start = (bf16[12,6,256,256]{3,2,1,0:T(8,128)(2,1)S(1)}, bf16[12,6,256,256]{3,2,1,0:T(8,128)(2,1)}, u32[]{:S(2)}) copy-start(bf16[12,6,256,256]{3,2,1,0:T(8,128)(2,1)} %blocks.3) | copy-start | bytes 28311556
  0.7 38.2 %copy-start.2 = (s32[12,6]{0,1:T(8,128)S(1)}, s32[12,6]{0,1:T(8,128)}, u32[]{:S(2)}) copy-start(s32[12,6]{0,1:T(8,128)} %param.5) | copy-start | bytes 868
